TPU v7x, 256 devices: a whole 4x4x8 slice. The times are simulated.
256 devices in a mesh: group: 8 (over y, core), dom: 32 (over z, x).
Axes of the slice: x: 4, y: 4, z: 8, core: 2. Of those that a mesh axis runs over, the one named last changes fastest.
Arguments:
- node_feats: bfloat16 [524288, 512], P(('group', 'dom')), may hold values from -36 to 36
- send_rows: int32 [256, 32, 32], P(('group', 'dom')), may hold values from 0 to 2047
- hub_rows: int32 [256, 8], P(('group', 'dom')), may hold values from 0 to 2047
- neighbours: int32 [524288, 16], P(('group', 'dom')), may hold values from 0 to 5119, as said below
- w_self: bfloat16 [512, 512], replicated, may hold values from -0.25 to 0.25
- w_neigh: bfloat16 [512, 512], replicated, may hold values from -0.25 to 0.25
- w_head: bfloat16 [512, 128], replicated, may hold values from -1.5 to 1.5
- s_first: bfloat16 [512, 512], replicated, may hold values from -0.25 to 0.25
- s_second: bfloat16 [512, 128], replicated, may hold values from -1.5 to 1.5
Outputs:
- teacher_hidden: bfloat16 [524288, 512], P(('group', 'dom'))
- grad_first: float32 [512, 512], replicated
- grad_second: float32 [512, 128], replicated
Inputs may be any that keep to these rules, and one draw needn't show every extreme that they name: `neighbours`: entries below 2048 are local rows; entries from 2048 to 3071 name halo rows, and from a given peer only its first rows, up to 32; the rest name hubs.
All inputs are finite; a program needn't handle non-finite values.
Results may differ from a plain program's by a relative error of at most 0.0025.
Values may be sent and summed in bfloat16 or wider, within the bound.
No kernel may reach another device: no remote copies, remote signals or barrier semaphores. Data moves between devices by JAX's collectives and lax.ppermute only.
A program may use at most 128 MiB of HBM per device.

v0:
```python
import jax
import jax.numpy as jnp
from jax import lax
from jax.sharding import PartitionSpec as P

DEG = 16
TEMPER = 2.0


def local_layer(feats, table, nbr, w_self, w_neigh, w_head, s_first, s_second, scale):
    rows = feats.shape[0]
    block = min(512, rows)

    def agg_block(index):
        picked = table[index].astype(jnp.float32)
        return (jnp.sum(picked, axis=1) / DEG).astype(jnp.bfloat16)

    agg = lax.map(agg_block, nbr.reshape(rows // block, block, DEG)).reshape(rows, feats.shape[1])
    pre = jnp.dot(feats, w_self, preferred_element_type=jnp.float32) + jnp.dot(
        agg, w_neigh, preferred_element_type=jnp.float32
    )
    hidden = jax.nn.relu(pre).astype(jnp.bfloat16)
    t_logits = jnp.dot(hidden, w_head, preferred_element_type=jnp.float32)
    s_pre = jnp.dot(feats, s_first, preferred_element_type=jnp.float32)
    s_hidden = jax.nn.relu(s_pre).astype(jnp.bfloat16)
    s_logits = jnp.dot(s_hidden, s_second, preferred_element_type=jnp.float32)
    p_teach = jax.nn.softmax(t_logits / TEMPER, axis=-1)
    p_stud = jax.nn.softmax(s_logits / TEMPER, axis=-1)
    delta = (TEMPER * (p_stud - p_teach) * scale).astype(jnp.bfloat16)
    g_second = jnp.dot(s_hidden.T, delta, preferred_element_type=jnp.float32)
    back = jnp.dot(delta, s_second.T, preferred_element_type=jnp.float32)
    back = jnp.where(s_pre > 0, back, 0.0).astype(jnp.bfloat16)
    g_first = jnp.dot(feats.T, back, preferred_element_type=jnp.float32)
    return (hidden, g_first, g_second)


def per_device(
    node_feats, send_rows, hub_rows, neighbours, w_self, w_neigh, w_head, s_first, s_second
):
    rows = node_feats.shape[0]
    width = node_feats.shape[1]
    outgoing = node_feats[send_rows[0]]
    received = lax.all_to_all(outgoing, "dom", split_axis=0, concat_axis=0, tiled=True)
    halo = received.reshape(-1, width)
    own_hubs = node_feats[hub_rows[0]]
    hubs = lax.all_gather(own_hubs, ("group", "dom"), axis=0, tiled=True)
    table = jnp.concatenate([node_feats, halo, hubs], axis=0)
    total_nodes = rows * lax.axis_size("group") * lax.axis_size("dom")
    scale = 1.0 / jnp.sqrt(jnp.float32(total_nodes))
    hidden, g_first, g_second = local_layer(
        node_feats, table, neighbours, w_self, w_neigh, w_head, s_first, s_second, scale
    )
    grad_first, grad_second = lax.psum((g_first, g_second), ("group", "dom"))
    return (hidden, grad_first, grad_second)


def solution(mesh):
    return jax.shard_map(
        per_device,
        mesh=mesh,
        in_specs=(
            P(("group", "dom"), None),
            P(("group", "dom"), None, None),
            P(("group", "dom"), None),
            P(("group", "dom"), None),
            P(),
            P(),
            P(),
            P(),
            P(),
        ),
        out_specs=(P(("group", "dom"), None), P(), P()),
        check_vma=False,
    )
```

profile of v0, /device:TPU:2, one launch (start us, length us, event | category | flops | bytes accessed | tf_op | source)
XLA Modules:
  0.0 601.0 jit_solution(7167910912744096948)
XLA Ops:
  7.2 0.0 copy-start
  7.2 0.0 all-gather.3.cloned.1.call-start
  7.2 0.7 fusion.7
  7.9 3.0 gather_fusion.2
  11.0 0.0 all-gather.3.cloned.1.call-update
  11.0 0.7 compare_select_fusion.1
  11.7 0.1 reshape.129
  11.8 0.0 copy-start.9
  11.8 7.1 %gather_fusion.1 = bf16[1024,512]{1,0:T(8,128)(2,1)} fusion(bf16[2048,512]{1,0:T(8,128)(2,1)} %param.11, s32[1024]{0:T(1024)S(1)} %broadcast_clamp_fusion.1), kind=kCustom, calls=%fused_computation.1 | custom fusion | bytes 2101248 | tf_op jit(solution)/shard_map/gather | solution.py:42
  18.9 11.7 %all-to-all-start = ((bf16[32,32,512]{2,1,0:T(8,128)(2,1)}), bf16[32,32,512]{2,1,0:T(8,128)(2,1)}, u32[]{:S(2)}, u32[]{:S(2)}) async-start(bf16[32,32,512]{2,1,0:T(8,128)(2,1)} %bitcast.43), calls=%async_computation | async-start | bytes 2097152 | tf_op jit(solution)/shard_map/all_to_all | solution.py:43
  30.6 0.0 all-reduce.3.cloned.1.call-start
  30.6 0.0 copy-done.9
  30.6 1.3 copy.15
  31.9 0.0 copy-done
  31.9 0.0 copy-done.1
  32.0 1.2 fusion.14
  33.2 0.0 copy-start.2
  33.2 1.9 copy-done.2
  35.1 0.0 copy-done.11
  35.1 1.8 fusion.12
  37.0 0.0 copy-done.7
  37.0 3.2 fusion.13
  40.2 18.6 %all-to-all-done = bf16[32,32,512]{2,1,0:T(8,128)(2,1)} async-done(((bf16[32,32,512]{2,1,0:T(8,128)(2,1)}), bf16[32,32,512]{2,1,0:T(8,128)(2,1)}, u32[]{:S(2)}, u32[]{:S(2)}) %all-to-all-start) | async-done | bytes 1048608 | tf_op jit(solution)/shard_map/all_to_all | solution.py:43
  58.8 61.9 %all-gather.3.cloned.1.call-done = bf16[2048,512]{1,0:T(8,128)(2,1)} async-done(((bf16[8,512]{1,0:T(8,128)(2,1)}), bf16[2048,512]{1,0:T(8,128)(2,1)}) %all-gather.3.cloned.1.call-update) | async-done | bytes 2097168 | tf_op jit(solution)/shard_map/all_gather | solution.py:46
  120.7 4.6 pad_maximum_fusion
  125.3 188.4 %while.10 = (s32[]{:T(128)}, bf16[4,512,512]{2,1,0:T(8,128)(2,1)}, s32[4,512,16]{2,1,0:T(8,128)}, bf16[5120,512]{1,0:T(8,128)(2,1)}, s32[]{:T(128)}) while((s32[]{:T(128)}, bf16[4,512,512]{2,1,0:T(8,128)(2,1)}, s32[4,512,16]{2,1,0:T(8,128)}, bf16[5120,512]{1,0:T(8,128)(2,1)}, s32[]{:T(128)}) %tuple.37), condition=%wide.region_2.3_spmd, body=%wide.region_0.2_spmd.sunk | while | flops 8683522 | bytes 28016716 | solution.py:18
  125.3 1.0 compare_select_fusion.4
  126.3 0.1 reshape.152
  126.5 37.0 %gather_fusion = bf16[8192,512]{1,0:T(8,128)(2,1)} fusion(bf16[5120,512]{1,0:T(8,128)(2,1)} %get-tuple-element.90, s32[8192]{0:T(1024)S(1)} %broadcast_clamp_fusion.3), kind=kCustom, calls=%fused_computation.clone.1 | custom fusion | bytes 16809984 | tf_op jit(solution)/shard_map/while/body/eval_jaxpr/gather | solution.py:15
  163.5 8.0 %convert_reduce_fusion.2 = f32[512,512]{1,0:T(8,128)S(1)} fusion(bf16[8192,512]{1,0:T(8,128)(2,1)} %gather_fusion), kind=kLoop, calls=%fused_computation.3.clone.1 | loop fusion | flops 8126464 | bytes 9437184 | tf_op jit(solution)/shard_map/while/body/eval_jaxpr/reduce_sum | solution.py:16
  171.5 0.9 fusion.27
  172.4 1.0 compare_select_fusion.4
  173.4 0.1 reshape.152
  173.6 37.0 %gather_fusion = bf16[8192,512]{1,0:T(8,128)(2,1)} fusion(bf16[5120,512]{1,0:T(8,128)(2,1)} %get-tuple-element.90, s32[8192]{0:T(1024)S(1)} %broadcast_clamp_fusion.3), kind=kCustom, calls=%fused_computation.clone.1 | custom fusion | bytes 16809984 | tf_op jit(solution)/shard_map/while/body/eval_jaxpr/gather | solution.py:15
  210.6 8.0 %convert_reduce_fusion.2 = f32[512,512]{1,0:T(8,128)S(1)} fusion(bf16[8192,512]{1,0:T(8,128)(2,1)} %gather_fusion), kind=kLoop, calls=%fused_computation.3.clone.1 | loop fusion | flops 8126464 | bytes 9437184 | tf_op jit(solution)/shard_map/while/body/eval_jaxpr/reduce_sum | solution.py:16
  218.6 0.9 fusion.27
  219.5 1.0 compare_select_fusion.4
  220.5 0.1 reshape.152
  220.7 37.0 %gather_fusion = bf16[8192,512]{1,0:T(8,128)(2,1)} fusion(bf16[5120,512]{1,0:T(8,128)(2,1)} %get-tuple-element.90, s32[8192]{0:T(1024)S(1)} %broadcast_clamp_fusion.3), kind=kCustom, calls=%fused_computation.clone.1 | custom fusion | bytes 16809984 | tf_op jit(solution)/shard_map/while/body/eval_jaxpr/gather | solution.py:15
  257.7 8.0 %convert_reduce_fusion.2 = f32[512,512]{1,0:T(8,128)S(1)} fusion(bf16[8192,512]{1,0:T(8,128)(2,1)} %gather_fusion), kind=kLoop, calls=%fused_computation.3.clone.1 | loop fusion | flops 8126464 | bytes 9437184 | tf_op jit(solution)/shard_map/while/body/eval_jaxpr/reduce_sum | solution.py:16
  265.7 0.9 fusion.27
  266.6 1.0 compare_select_fusion.4
  267.6 0.1 reshape.152
  267.8 37.0 %gather_fusion = bf16[8192,512]{1,0:T(8,128)(2,1)} fusion(bf16[5120,512]{1,0:T(8,128)(2,1)} %get-tuple-element.90, s32[8192]{0:T(1024)S(1)} %broadcast_clamp_fusion.3), kind=kCustom, calls=%fused_computation.clone.1 | custom fusion | bytes 16809984 | tf_op jit(solution)/shard_map/while/body/eval_jaxpr/gather | solution.py:15
  304.8 8.0 %convert_reduce_fusion.2 = f32[512,512]{1,0:T(8,128)S(1)} fusion(bf16[8192,512]{1,0:T(8,128)(2,1)} %gather_fusion), kind=kLoop, calls=%fused_computation.3.clone.1 | loop fusion | flops 8126464 | bytes 9437184 | tf_op jit(solution)/shard_map/while/body/eval_jaxpr/reduce_sum | solution.py:16
  312.8 0.9 fusion.27
  313.7 0.0 copy-done.8
  313.7 4.2 maximum_convert_fusion.1
  317.9 0.0 copy-start.4
  317.9 1.3 copy-done.4
  319.2 0.0 copy-done.10
  319.2 0.8 fusion.11
  320.1 0.0 copy-start.5
  320.1 0.0 copy-done.6
  320.1 0.3 fusion.4
  320.4 0.6 copy-done.5
  321.0 0.8 copy-done.3
  321.8 1.6 fusion.6
  323.4 0.0 copy-done.12
  323.4 6.0 %fusion.3 = f32[512,512]{0,1:T(8,128)} fusion(bf16[2048,512]{1,0:T(8,128)(2,1)S(1)} %copy-done.1, f32[2048,512]{1,0:T(8,128)} %copy-done.2, bf16[512,128]{1,0:T(8,128)(2,1)S(1)} %copy-done.12, f32[2048,128]{0,1:T(8,128)} %get-tuple-element.49, f32[2048,128]{0,1:T(8,128)} %copy-done.5, f32[2048]{0:T(1024)S(1)} %get-tuple-element.51, ...), kind=kOutput, calls=%fused_computation.16 | convolution fusion | flops 1347158016 | bytes 9601024 | tf_op jit(solution)/shard_map/dot_general | solution.py:33
  329.4 0.0 all-reduce.3.cloned.1.call-update
  329.4 260.5 %all-reduce.3.cloned.1.call-done = (f32[512,512]{0,1:T(8,128)}, f32[512,128]{1,0:T(8,128)}) async-done(((f32[512,512]{0,1:T(8,128)}, f32[512,128]{1,0:T(8,128)}), (f32[512,512]{0,1:T(8,128)}, f32[512,128]{1,0:T(8,128)})) %all-reduce.3.cloned.1.call-update) | async-done | bytes 1310736 | tf_op jit(solution)/shard_map/psum | solution.py:53
  589.9 2.5 copy.14
  592.5 1.7 copy.27
  (15 shorter events, 0.1 us)
Async XLA Ops:
  7.2 24.8 %copy-start = (bf16[512,512]{1,0:T(8,128)(2,1)S(1)}, bf16[512,512]{1,0:T(8,128)(2,1)}, u32[]{:S(2)}) copy-start(bf16[512,512]{1,0:T(8,128)(2,1)} %param.18) | copy-start | bytes 1572868
  7.2 113.5 %all-gather.3.cloned.1.call-start = ((), (), s32[]{:S(2)}) async-start(), calls=%async_computation.1 | async-start | bytes 2105344 | tf_op jit(solution)/shard_map/all_gather | solution.py:46
  11.8 18.8 %copy-start.9 = (s32[2048,16]{0,1:T(8,128)S(1)}, s32[2048,16]{0,1:T(8,128)}, u32[]{:S(2)}) copy-start(s32[2048,16]{0,1:T(8,128)} %param.14) | copy-start | bytes 393220
  11.8 20.2 %copy-start.1 = (bf16[2048,512]{1,0:T(8,128)(2,1)S(1)}, bf16[2048,512]{1,0:T(8,128)(2,1)}, u32[]{:S(2)}) copy-start(bf16[2048,512]{1,0:T(8,128)(2,1)} %param.11) | copy-start | bytes 6291460
  18.9 39.9 %all-to-all-start = ((bf16[32,32,512]{2,1,0:T(8,128)(2,1)}), bf16[32,32,512]{2,1,0:T(8,128)(2,1)}, u32[]{:S(2)}, u32[]{:S(2)}) async-start(bf16[32,32,512]{2,1,0:T(8,128)(2,1)} %bitcast.43), calls=%async_computation | async-start | bytes 2097152 | tf_op jit(solution)/shard_map/all_to_all | solution.py:43
  30.6 559.4 %all-reduce.3.cloned.1.call-start = ((), (), s32[]{:S(2)}) async-start(), calls=%async_computation.2 | async-start | bytes 2621440 | tf_op jit(solution)/shard_map/psum | solution.py:53
  32.0 3.2 copy-start.11
  33.2 1.9 copy-start.2
  35.1 1.8 copy-start.7
  125.3 188.4 %copy-start.8 = (bf16[512,512]{1,0:T(8,128)(2,1)S(1)}, bf16[512,512]{1,0:T(8,128)(2,1)}, u32[]{:S(2)}) copy-start(bf16[512,512]{1,0:T(8,128)(2,1)} %param.16) | copy-start | bytes 1572868
  313.7 5.5 copy-start.10
  313.7 6.3 %copy-start.6 = (f32[2048,128]{0,1:T(8,128)S(1)}, f32[2048,128]{0,1:T(8,128)}, u32[]{:S(2)}) copy-start(f32[2048,128]{0,1:T(8,128)} %get-tuple-element.49) | copy-start | bytes 3145732
  317.9 1.3 copy-start.4
  319.2 2.6 copy-start.3
  320.1 1.0 copy-start.5
  321.8 1.6 copy-start.12
Sparse Core Ops, SparseCore 0:
  12.3 108.3 all-gather.2
  329.5 260.3 all-reduce.2
where the time goes:
time: 602 us; the launch traced here: 601 us
  waiting for transfers between devices  341 us (57%)
  local copies, waits for them, and re-layouts  169 us (28%)
  other arithmetic  46.2 us (8%)
  matrix products  18.9 us (3%)
  between operations  14.1 us (2%)
  starting transfers between devices  11.7 us (2%)
    psum x1, waiting for transfers between devices, per_device(): grad_first, grad_second = lax.psum((g_first, g_second), ('group', 'dom'))  261 us
    gather x4, local copies, waits for them, and re-layouts, agg_block(): picked = table[index].astype(jnp.float32)  148 us
    all_gather x1, waiting for transfers between devices, per_device(): hubs = lax.all_gather(own_hubs, ('group', 'dom'), axis=0, tiled=True)  61.9 us
    reduce_sum x4, other arithmetic, agg_block(): return (jnp.sum(picked, axis=1) / DEG).astype(jnp.bfloat16)  32.1 us
    all_to_all x1, waiting for transfers between devices, per_device(): lax.all_to_all(outgoing, 'dom', split_axis=0, concat_axis=0, tiled=True)  18.6 us
  transfers between devices with their start and end apart: 3, of which 3 were waited for; matrix products, arithmetic and copies ran while one was open for 3% of the time, Pallas kernels for 0%

commit v1 on v0

--- a/solution.py
+++ b/solution.py
@@ -2,6 +2,7 @@
 import jax.numpy as jnp
 from jax import lax
 from jax.sharding import PartitionSpec as P
+from jax.lax import psum
 
 DEG = 16
 TEMPER = 2.0
@@ -50,7 +51,7 @@
     hidden, g_first, g_second = local_layer(
         node_feats, table, neighbours, w_self, w_neigh, w_head, s_first, s_second, scale
     )
-    grad_first, grad_second = lax.psum((g_first, g_second), ("group", "dom"))
+    grad_first, grad_second = psum(psum((g_first, g_second), axis_name="group"), axis_name="dom")
     return (hidden, grad_first, grad_second)
 
 

time: 602 us -> 563 us (0.935)
  waiting for transfers between devices: 341 us -> 301 us
    psum x1 -> x2, waiting for transfers between devices: 261 us -> 221 us  [the longest x1 153 us: per_device(): psum(psum((g_first, g_second), axis_name='group'), axis_name='dom')]
  transfers between devices with their start and end apart: 3 -> 4, of which waited for: 3 -> 4; matrix products, arithmetic and copies ran while one was open for 3% -> 3% of each run, Pallas kernels for 0% -> 0%
where the time goes in v1:
time: 563 us; the launch traced here: 561 us
  waiting for transfers between devices  301 us (53%)
  local copies, waits for them, and re-layouts  169 us (30%)
  other arithmetic  46.2 us (8%)
  matrix products  18.9 us (3%)
  between operations  13.8 us (2%)
  starting transfers between devices  11.8 us (2%)
    psum x1, waiting for transfers between devices, per_device(): psum(psum((g_first, g_second), axis_name='group'), axis_name='dom')  153 us
    gather x4, local copies, waits for them, and re-layouts, agg_block(): picked = table[index].astype(jnp.float32)  148 us
    psum x1, waiting for transfers between devices, per_device(): psum((g_first, g_second), axis_name='group')  67.7 us
    all_gather x1, waiting for transfers between devices, per_device(): hubs = lax.all_gather(own_hubs, ('group', 'dom'), axis=0, tiled=True)  61.9 us
    reduce_sum x4, other arithmetic, agg_block(): return (jnp.sum(picked, axis=1) / DEG).astype(jnp.bfloat16)  32.1 us
    all_to_all x1, waiting for transfers between devices, per_device(): lax.all_to_all(outgoing, 'dom', split_axis=0, concat_axis=0, tiled=True)  18.6 us
    all_to_all x1, starting transfers between devices, per_device(): lax.all_to_all(outgoing, 'dom', split_axis=0, concat_axis=0, tiled=True)  11.7 us
  transfers between devices with their start and end apart: 4, of which 4 were waited for; matrix products, arithmetic and copies ran while one was open for 3% of the time, Pallas kernels for 0%

profile of v1, /device:TPU:2, one launch (start us, length us, event | category | flops | bytes accessed | tf_op | source)
XLA Modules:
  0.0 561.0 jit_solution(6870264504949153211)
XLA Ops:
  7.2 0.0 copy-start
  7.2 0.0 all-gather.3.cloned.1.call-start
  7.2 0.7 fusion.7
  7.9 3.0 gather_fusion.2
  11.0 0.0 all-gather.3.cloned.1.call-update
  11.0 0.7 compare_select_fusion.1
  11.7 0.1 reshape.129
  11.8 7.1 %gather_fusion.1 = bf16[1024,512]{1,0:T(8,128)(2,1)} fusion(bf16[2048,512]{1,0:T(8,128)(2,1)} %param.11, s32[1024]{0:T(1024)S(1)} %broadcast_clamp_fusion.1), kind=kCustom, calls=%fused_computation.1 | custom fusion | bytes 2101248 | tf_op jit(solution)/shard_map/gather | solution.py:43
  18.9 11.7 %all-to-all-start = ((bf16[32,32,512]{2,1,0:T(8,128)(2,1)}), bf16[32,32,512]{2,1,0:T(8,128)(2,1)}, u32[]{:S(2)}, u32[]{:S(2)}) async-start(bf16[32,32,512]{2,1,0:T(8,128)(2,1)} %bitcast.43), calls=%async_computation | async-start | bytes 2097152 | tf_op jit(solution)/shard_map/all_to_all | solution.py:44
  30.6 0.0 all-reduce.7.cloned.1.call-start
  30.7 0.0 copy-done.9
  30.7 1.3 copy.15
  32.0 0.0 copy-done
  32.0 0.0 copy-done.1
  32.0 1.3 fusion.14
  33.2 0.0 copy-start.2
  33.2 1.9 copy-done.2
  35.2 0.0 copy-done.11
  35.2 1.8 fusion.12
  37.0 0.0 copy-done.7
  37.0 3.2 fusion.13
  40.2 18.6 %all-to-all-done = bf16[32,32,512]{2,1,0:T(8,128)(2,1)} async-done(((bf16[32,32,512]{2,1,0:T(8,128)(2,1)}), bf16[32,32,512]{2,1,0:T(8,128)(2,1)}, u32[]{:S(2)}, u32[]{:S(2)}) %all-to-all-start) | async-done | bytes 1048608 | tf_op jit(solution)/shard_map/all_to_all | solution.py:44
  58.8 61.9 %all-gather.3.cloned.1.call-done = bf16[2048,512]{1,0:T(8,128)(2,1)} async-done(((bf16[8,512]{1,0:T(8,128)(2,1)}), bf16[2048,512]{1,0:T(8,128)(2,1)}) %all-gather.3.cloned.1.call-update) | async-done | bytes 2097168 | tf_op jit(solution)/shard_map/all_gather | solution.py:47
  120.7 4.6 pad_maximum_fusion
  125.3 188.2 %while.10 = (s32[]{:T(128)}, bf16[4,512,512]{2,1,0:T(8,128)(2,1)}, s32[4,512,16]{2,1,0:T(8,128)}, bf16[5120,512]{1,0:T(8,128)(2,1)}, s32[]{:T(128)}) while((s32[]{:T(128)}, bf16[4,512,512]{2,1,0:T(8,128)(2,1)}, s32[4,512,16]{2,1,0:T(8,128)}, bf16[5120,512]{1,0:T(8,128)(2,1)}, s32[]{:T(128)}) %tuple.40), condition=%wide.region_2.3_spmd, body=%wide.region_0.2_spmd.sunk | while | flops 8683522 | bytes 28016716 | solution.py:19
  125.3 1.0 compare_select_fusion.4
  126.4 0.1 reshape.152
  126.5 37.0 %gather_fusion = bf16[8192,512]{1,0:T(8,128)(2,1)} fusion(bf16[5120,512]{1,0:T(8,128)(2,1)} %get-tuple-element.92, s32[8192]{0:T(1024)S(1)} %broadcast_clamp_fusion.3), kind=kCustom, calls=%fused_computation.clone.1 | custom fusion | bytes 16809984 | tf_op jit(solution)/shard_map/while/body/eval_jaxpr/gather | solution.py:16
  163.5 8.0 %convert_reduce_fusion.2 = f32[512,512]{1,0:T(8,128)S(1)} fusion(bf16[8192,512]{1,0:T(8,128)(2,1)} %gather_fusion), kind=kLoop, calls=%fused_computation.3.clone.1 | loop fusion | flops 8126464 | bytes 9437184 | tf_op jit(solution)/shard_map/while/body/eval_jaxpr/reduce_sum | solution.py:17
  171.5 0.9 fusion.27
  172.4 1.0 compare_select_fusion.4
  173.4 0.1 reshape.152
  173.6 37.0 %gather_fusion = bf16[8192,512]{1,0:T(8,128)(2,1)} fusion(bf16[5120,512]{1,0:T(8,128)(2,1)} %get-tuple-element.92, s32[8192]{0:T(1024)S(1)} %broadcast_clamp_fusion.3), kind=kCustom, calls=%fused_computation.clone.1 | custom fusion | bytes 16809984 | tf_op jit(solution)/shard_map/while/body/eval_jaxpr/gather | solution.py:16
  210.5 8.0 %convert_reduce_fusion.2 = f32[512,512]{1,0:T(8,128)S(1)} fusion(bf16[8192,512]{1,0:T(8,128)(2,1)} %gather_fusion), kind=kLoop, calls=%fused_computation.3.clone.1 | loop fusion | flops 8126464 | bytes 9437184 | tf_op jit(solution)/shard_map/while/body/eval_jaxpr/reduce_sum | solution.py:17
  218.6 0.9 fusion.27
  219.5 1.0 compare_select_fusion.4
  220.5 0.1 reshape.152
  220.6 37.0 %gather_fusion = bf16[8192,512]{1,0:T(8,128)(2,1)} fusion(bf16[5120,512]{1,0:T(8,128)(2,1)} %get-tuple-element.92, s32[8192]{0:T(1024)S(1)} %broadcast_clamp_fusion.3), kind=kCustom, calls=%fused_computation.clone.1 | custom fusion | bytes 16809984 | tf_op jit(solution)/shard_map/while/body/eval_jaxpr/gather | solution.py:16
  257.6 8.0 %convert_reduce_fusion.2 = f32[512,512]{1,0:T(8,128)S(1)} fusion(bf16[8192,512]{1,0:T(8,128)(2,1)} %gather_fusion), kind=kLoop, calls=%fused_computation.3.clone.1 | loop fusion | flops 8126464 | bytes 9437184 | tf_op jit(solution)/shard_map/while/body/eval_jaxpr/reduce_sum | solution.py:17
  265.6 0.9 fusion.27
  266.5 1.0 compare_select_fusion.4
  267.5 0.1 reshape.152
  267.7 37.0 %gather_fusion = bf16[8192,512]{1,0:T(8,128)(2,1)} fusion(bf16[5120,512]{1,0:T(8,128)(2,1)} %get-tuple-element.92, s32[8192]{0:T(1024)S(1)} %broadcast_clamp_fusion.3), kind=kCustom, calls=%fused_computation.clone.1 | custom fusion | bytes 16809984 | tf_op jit(solution)/shard_map/while/body/eval_jaxpr/gather | solution.py:16
  304.6 8.0 %convert_reduce_fusion.2 = f32[512,512]{1,0:T(8,128)S(1)} fusion(bf16[8192,512]{1,0:T(8,128)(2,1)} %gather_fusion), kind=kLoop, calls=%fused_computation.3.clone.1 | loop fusion | flops 8126464 | bytes 9437184 | tf_op jit(solution)/shard_map/while/body/eval_jaxpr/reduce_sum | solution.py:17
  312.7 0.9 fusion.27
  313.6 0.0 copy-done.8
  313.6 4.2 maximum_convert_fusion.1
  317.8 0.0 copy-start.4
  317.8 1.3 copy-done.4
  319.1 0.0 copy-done.10
  319.1 0.8 fusion.11
  319.9 0.0 copy-start.5
  319.9 0.3 fusion.4
  320.3 0.6 copy-done.5
  320.9 0.8 copy-done.3
  321.6 1.6 fusion.6
  323.2 6.0 %fusion.3 = f32[512,512]{0,1:T(8,128)} fusion(bf16[2048,512]{1,0:T(8,128)(2,1)S(1)} %copy-done.1, f32[2048,512]{1,0:T(8,128)} %copy-done.2, bf16[512,128]{1,0:T(8,128)(2,1)S(1)} %copy-done.12, f32[2048,128]{0,1:T(8,128)} %get-tuple-element.51, f32[2048,128]{0,1:T(8,128)} %copy-done.5, f32[2048]{0:T(1024)S(1)} %get-tuple-element.53, ...), kind=kOutput, calls=%fused_computation.16 | convolution fusion | flops 1347158016 | bytes 9601024 | tf_op jit(solution)/shard_map/dot_general | solution.py:34
  329.2 0.0 all-reduce.7.cloned.1.call-update
  329.3 0.0 all-reduce.5.cloned.1.call-start
  329.3 67.7 %all-reduce.7.cloned.1.call-done = (f32[512,512]{0,1:T(8,128)}, f32[512,128]{1,0:T(8,128)}) async-done(((f32[512,512]{0,1:T(8,128)}, f32[512,128]{1,0:T(8,128)}), (f32[512,512]{0,1:T(8,128)}, f32[512,128]{1,0:T(8,128)})) %all-reduce.7.cloned.1.call-update) | async-done | bytes 1310736 | tf_op jit(solution)/shard_map/psum | solution.py:54
  397.0 0.0 all-reduce.5.cloned.1.call-update
  397.0 153.2 %all-reduce.5.cloned.1.call-done = (f32[512,512]{0,1:T(8,128)}, f32[512,128]{1,0:T(8,128)}) async-done(((f32[512,512]{0,1:T(8,128)}, f32[512,128]{1,0:T(8,128)}), (f32[512,512]{0,1:T(8,128)}, f32[512,128]{1,0:T(8,128)})) %all-reduce.5.cloned.1.call-update) | async-done | bytes 1310736 | tf_op jit(solution)/shard_map/psum | solution.py:54
  550.2 2.5 copy.14
  552.8 1.7 copy.29
  (18 shorter events, 0.1 us)
Async XLA Ops:
  7.2 24.8 %copy-start = (bf16[512,512]{1,0:T(8,128)(2,1)S(1)}, bf16[512,512]{1,0:T(8,128)(2,1)}, u32[]{:S(2)}) copy-start(bf16[512,512]{1,0:T(8,128)(2,1)} %param.18) | copy-start | bytes 1572868
  7.2 113.6 %all-gather.3.cloned.1.call-start = ((), (), s32[]{:S(2)}) async-start(), calls=%async_computation.1 | async-start | bytes 2105344 | tf_op jit(solution)/shard_map/all_gather | solution.py:47
  11.8 18.9 %copy-start.9 = (s32[2048,16]{0,1:T(8,128)S(1)}, s32[2048,16]{0,1:T(8,128)}, u32[]{:S(2)}) copy-start(s32[2048,16]{0,1:T(8,128)} %param.14) | copy-start | bytes 393220
  11.8 20.2 %copy-start.1 = (bf16[2048,512]{1,0:T(8,128)(2,1)S(1)}, bf16[2048,512]{1,0:T(8,128)(2,1)}, u32[]{:S(2)}) copy-start(bf16[2048,512]{1,0:T(8,128)(2,1)} %param.11) | copy-start | bytes 6291460
  18.9 39.9 %all-to-all-start = ((bf16[32,32,512]{2,1,0:T(8,128)(2,1)}), bf16[32,32,512]{2,1,0:T(8,128)(2,1)}, u32[]{:S(2)}, u32[]{:S(2)}) async-start(bf16[32,32,512]{2,1,0:T(8,128)(2,1)} %bitcast.43), calls=%async_computation | async-start | bytes 2097152 | tf_op jit(solution)/shard_map/all_to_all | solution.py:44
  30.6 366.4 %all-reduce.7.cloned.1.call-start = ((), (), s32[]{:S(2)}) async-start(), calls=%async_computation.3 | async-start | bytes 2621440 | tf_op jit(solution)/shard_map/psum | solution.py:54
  32.0 3.2 copy-start.11
  33.2 1.9 copy-start.2
  35.2 1.8 copy-start.7
  125.3 188.2 %copy-start.8 = (bf16[512,512]{1,0:T(8,128)(2,1)S(1)}, bf16[512,512]{1,0:T(8,128)(2,1)}, u32[]{:S(2)}) copy-start(bf16[512,512]{1,0:T(8,128)(2,1)} %param.16) | copy-start | bytes 1572868
  313.6 5.5 copy-start.10
  313.6 6.3 %copy-start.6 = (f32[2048,128]{0,1:T(8,128)S(1)}, f32[2048,128]{0,1:T(8,128)}, u32[]{:S(2)}) copy-start(f32[2048,128]{0,1:T(8,128)} %get-tuple-element.51) | copy-start | bytes 3145732
  317.8 1.3 copy-start.4
  319.1 2.6 copy-start.3
  319.9 1.0 copy-start.5
  321.6 1.6 copy-start.12
  329.3 221.0 %all-reduce.5.cloned.1.call-start = ((), (), s32[]{:S(2)}) async-start(), calls=%async_computation.2 | async-start | bytes 2621440 | tf_op jit(solution)/shard_map/psum | solution.py:54
Sparse Core Ops, SparseCore 0:
  12.3 108.4 all-gather.2
  329.4 67.5 all-reduce.6
  400.5 149.6 all-reduce.4
